TPU v7x, 32 devices: a whole 2x2x4 slice. The times are simulated.
32 devices in a mesh: gx: 8 (over z, core), gy: 4 (over y, x).
Axes of the slice: x: 2, y: 2, z: 4, core: 2. Of those that a mesh axis runs over, the one named last changes fastest.
Arguments:
- adj_voltage: float32 [8, 256, 128], P('gx', 'gy'), may hold values from -6 to 6
- adj_gating: float32 [8, 256, 128], P('gx', 'gy'), may hold values from -1.2 to 1.2
- fwd_voltage: bfloat16 [2, 8, 256, 128], P(None, 'gx', 'gy'), may hold values from -0.099609375 to 1.09375
- fwd_gating: bfloat16 [2, 8, 256, 128], P(None, 'gx', 'gy'), may hold values from 0 to 2
- region_labels: int32 [8, 256, 1], P('gx', 'gy'), may hold values from 0 to 7
- region_axial: float32 [2, 8], replicated, may hold values from 0.6 to 3
- region_shear: float32 [8], replicated, may hold values from -0.5 to 0.5
- block_rate: float32 [2], replicated, may hold values from 8 to 32
- block_inverse: float32 [2, 128, 128], replicated, as said below
Outputs:
- voltage_adjoint: float32 [8, 256, 128], P('gx', 'gy')
- gating_adjoint: float32 [8, 256, 128], P('gx', 'gy')
Inputs may be any that keep to these rules, and one draw needn't show every extreme that they name: block_inverse[b] is the inverse of the 128 x 128 tridiagonal matrix with diagonal 1 + 2 block_rate[b] and off-diagonals -block_rate[b].
All inputs are finite; a program needn't handle non-finite values.
Results may differ from a plain program's by a relative error of at most 0.00065.
Values sent between devices are 32-bit elements; how exact they have to be, the bound alone decides.
No kernel may reach another device: no remote copies, remote signals or barrier semaphores. Data moves between devices by JAX's collectives and lax.ppermute only.
A program may use at most 64 MiB of HBM per device.

v0:
```python
import jax
import jax.numpy as jnp
from jax import lax
from jax.sharding import PartitionSpec as P

STEPS = 2
SWEEPS = 11
ZB = 128
LB = 128
FULL_PRECISION = lax.Precision.HIGHEST
TIME_STEP = 0.2
RECOVERY_RATE = 0.25
EXCITATION = 8.0
THRESHOLD = 0.15


def with_halo(x, sides, width):
    for axis, dim in sides:
        size, length = (lax.axis_size(axis), x.shape[dim])
        up = [(i, (i + 1) % size) for i in range(size - 1)]
        down = [(j, i) for i, j in up]
        last = lax.slice_in_dim(x, length - width, length, axis=dim)
        leading = lax.slice_in_dim(x, 0, width, axis=dim)
        before = lax.ppermute(last, axis, up)
        after = lax.ppermute(leading, axis, down)
        x = jnp.concatenate([before, x, after], axis=dim)
    return x


def lookup(labels, lookup_table):
    levels = jnp.arange(lookup_table.shape[0], dtype=jnp.int32)
    return jnp.sum(jnp.where(labels[..., None] == levels, lookup_table, 0.0), axis=-1)


def expand_blocks(block_values):
    block_shape = block_values.shape
    wide_form = jnp.broadcast_to(block_values[..., None], block_shape + (LB,))
    return wide_form.reshape(block_shape[0], block_shape[1], block_shape[2] * LB)


def coefficients(labels, region_axial, region_shear):
    tissue_block = (labels > 0).astype(jnp.float32)
    return (
        expand_blocks(tissue_block),
        expand_blocks(lookup(labels, region_axial[0]) * tissue_block),
        expand_blocks(lookup(labels, region_axial[1]) * tissue_block),
        expand_blocks(lookup(labels, region_shear) * tissue_block),
    )


def couplings(block_rate):
    zero_rate = jnp.zeros((1,), jnp.float32)
    inner_rate = jnp.minimum(block_rate[:-1], block_rate[1:])
    return (jnp.concatenate([zero_rate, inner_rate]), jnp.concatenate([inner_rate, zero_rate]))


def line_solve(line_cells, block_rate, block_inverse):
    item_count, length_cells, across = line_cells.shape
    blocks_count = length_cells // ZB
    shaped = line_cells.reshape(item_count, blocks_count, ZB, across)
    below_rate, after_rate = couplings(block_rate)
    base_blocks = jnp.einsum("bij,xbjy->xbiy", block_inverse, shaped, precision=FULL_PRECISION)
    zero_row = jnp.zeros((item_count, 1, across), jnp.float32)
    middle = jnp.zeros((item_count, blocks_count, ZB - 2, across), jnp.float32)

    def sweep_once(sweep_index, current):
        first_cells = current[:, :, 0, :]
        last_cells = current[:, :, ZB - 1, :]
        from_below = (
            jnp.concatenate([zero_row, last_cells[:, :-1, :]], axis=1) * below_rate[None, :, None]
        )
        from_above = (
            jnp.concatenate([first_cells[:, 1:, :], zero_row], axis=1) * after_rate[None, :, None]
        )
        coupling = jnp.concatenate(
            [from_below[:, :, None, :], middle, from_above[:, :, None, :]], axis=2
        )
        updated = jnp.einsum(
            "bij,xbjy->xbiy", block_inverse, shaped + coupling, precision=FULL_PRECISION
        )
        return updated

    current = lax.fori_loop(0, SWEEPS, sweep_once, base_blocks)
    return current.reshape(item_count, length_cells, across)


def cross_terms(ext_xx, ext_yy, ext_xy):
    pad_y = ((0, 0), (0, 0), (1, 1))
    ext_yy = jnp.pad(ext_yy, pad_y)
    ext_xy = jnp.pad(ext_xy, pad_y)
    term_xx = ext_xx[2:] - 2.0 * ext_xx[1:-1] + ext_xx[:-2]
    term_yy = ext_yy[1:-1, :, 2:] - 2.0 * ext_yy[1:-1, :, 1:-1] + ext_yy[1:-1, :, :-2]
    term_xy = (
        ext_xy[2:, :, 2:] - ext_xy[2:, :, :-2] - ext_xy[:-2, :, 2:] + ext_xy[:-2, :, :-2]
    ) * 0.25
    return term_xx + term_yy + 2.0 * term_xy


def per_device(
    adj_voltage,
    adj_gating,
    fwd_voltage,
    fwd_gating,
    region_labels,
    region_axial,
    region_shear,
    block_rate,
    block_inverse,
):
    groups = lax.axis_size("gy")
    row_count, depth_cells, width_cells = adj_voltage.shape
    narrow = width_cells // groups
    tissue, coef_xx, coef_yy, coef_xy = coefficients(region_labels, region_axial, region_shear)
    adjoint_v = adj_voltage
    adjoint_w = adj_gating
    for step_index in range(STEPS):
        later_index = STEPS - 1 - step_index
        outgoing = adjoint_v.reshape(row_count, 1, depth_cells, groups, narrow)
        pieces = lax.all_to_all(outgoing, "gy", split_axis=3, concat_axis=1, tiled=True)
        item_count = pieces.shape[0]
        line_cells = pieces.reshape(item_count, groups * depth_cells, narrow)
        solved_lines = line_solve(line_cells, block_rate, block_inverse)
        returned_form = solved_lines.reshape(item_count, groups, depth_cells, 1, narrow)
        returned = lax.all_to_all(returned_form, "gy", split_axis=1, concat_axis=3, tiled=True)
        solved = returned.reshape(item_count, depth_cells, width_cells)
        stacked = jnp.stack([coef_xx * solved, coef_yy * solved, coef_xy * solved])
        extended = with_halo(stacked, (("gx", 1),), 1)
        spread_term = cross_terms(extended[0], extended[1], extended[2])
        voltage_now = fwd_voltage[later_index].astype(jnp.float32)
        gating_now = fwd_gating[later_index].astype(jnp.float32)
        ionic_slope = (
            EXCITATION
            * (-3.0 * voltage_now * voltage_now + 2.0 * (1.0 + THRESHOLD) * voltage_now - THRESHOLD)
            - gating_now
        )
        next_v = tissue * (
            solved
            + TIME_STEP * spread_term
            + TIME_STEP * ionic_slope * solved
            + TIME_STEP * RECOVERY_RATE * EXCITATION * adjoint_w
        )
        adjoint_w = tissue * (
            (1.0 - TIME_STEP * RECOVERY_RATE) * adjoint_w - TIME_STEP * voltage_now * solved
        )
        adjoint_v = next_v
    return (adjoint_v, adjoint_w)


def solution(mesh):
    return jax.shard_map(
        per_device,
        mesh=mesh,
        in_specs=(
            P("gx", "gy", None),
            P("gx", "gy", None),
            P(None, "gx", "gy", None),
            P(None, "gx", "gy", None),
            P("gx", "gy", None),
            P(),
            P(),
            P(),
            P(),
        ),
        out_specs=(P("gx", "gy", None), P("gx", "gy", None)),
        check_vma=False,
    )
```

profile of v0, /device:TPU:1, one launch (start us, length us, event | category | flops | bytes accessed | tf_op | source)
XLA Modules:
  0.0 79.6 jit_solution(2943020983780482412)
XLA Ops:
  0.6 0.8 %copy.73 = f32[1,64,128]{1,2,0:T(8,128)S(1)} copy(f32[1,64,128]{2,1,0:T(8,128)} %param.13) | data formatting | bytes 65536 | tf_op args[0]
  1.5 0.7 reshape.981
  2.2 4.4 %all-to-all-start = ((f32[4,1,2048]{2,1,0:T(1,128)}), f32[4,1,2048]{2,1,0:T(1,128)S(1)}, u32[]{:S(2)}, u32[]{:S(2)}) async-start(f32[4,1,2048]{2,1,0:T(1,128)} %reshape.981), calls=%async_computation | async-start | bytes 65536 | tf_op jit(solution)/shard_map/all_to_all | solution.py:119
  7.3 0.7 copy-done.3
  10.7 0.7 reduce.11
  12.8 9.9 %while.20 = (s32[]{:T(128)}, f32[1,2,128,32]{2,3,1,0:T(8,128)S(1)}, f32[1,2,128,32]{2,3,1,0:T(8,128)S(1)}, f32[2]{0:T(128)S(1)}, f32[2]{0:T(128)S(1)}, /*index=5...) while((s32[]{:T(128)}, f32[1,2,128,32]{2,3,1,0:T(8,128)S(1)}, f32[1,2,128,32]{2,3,1,0:T(8,128)S(1)}, ...), condition=%wide.region_1.2_spmd, body=%wide.region_0.1_spmd.sunk | while | flops 12607618 | bytes 202597 | solution.py:83
  22.9 0.7 reshape.983
  23.6 3.6 %all-to-all-start.1 = ((f32[4,1,2048]{2,1,0:T(1,128)}), f32[4,1,2048]{2,1,0:T(1,128)S(1)}, u32[]{:S(2)}, u32[]{:S(2)}) async-start(f32[4,1,2048]{2,1,0:T(1,128)} %reshape.983), calls=%async_computation.1 | async-start | bytes 65536 | tf_op jit(solution)/shard_map/all_to_all | solution.py:124
  27.3 3.6 %all-to-all-done.1 = f32[4,1,2048]{2,1,0:T(1,128)S(1)} async-done(((f32[4,1,2048]{2,1,0:T(1,128)}), f32[4,1,2048]{2,1,0:T(1,128)S(1)}, u32[]{:S(2)}, u32[]{:S(2)}) %all-to-all-start.1) | async-done | bytes 32800 | tf_op jit(solution)/shard_map/all_to_all | solution.py:124
  30.9 0.7 reduce.12
  31.7 4.8 %collective-permute-start = (f32[3,1,64,128]{2,3,1,0:T(8,128)S(1)}, f32[3,1,64,128]{2,3,1,0:T(8,128)S(1)}, u32[]{:S(2)}, u32[]{:S(2)}) collective-permute-start(f32[3,1,64,128]{2,3,1,0:T(8,128)S(1)} %pad_maximum_fusion.8), channel_id=1, source_target_pairs={{4,0},{8,4},{12,8},{16,12},{20,16},{24,20},{28,24},{5,1},{9,5},{13... | collective-permute-start | bytes 294920 | tf_op jit(solution)/shard_map/ppermute | solution.py:25
  36.5 3.1 %collective-permute-start.1 = (f32[3,1,64,128]{2,3,1,0:T(8,128)S(1)}, f32[3,1,64,128]{2,3,1,0:T(8,128)S(1)}, u32[]{:S(2)}, u32[]{:S(2)}) collective-permute-start(f32[3,1,64,128]{2,3,1,0:T(8,128)S(1)} %pad_maximum_fusion.8), channel_id=1, source_target_pairs={{0,4},{4,8},{8,12},{12,16},{16,20},{20,24},{24,28},{1,5},{5,9},{9,... | collective-permute-start | bytes 294920 | tf_op jit(solution)/shard_map/ppermute | solution.py:24
  41.0 1.2 %collective-permute-done.1 = f32[3,1,64,128]{2,3,1,0:T(8,128)S(1)} collective-permute-done((f32[3,1,64,128]{2,3,1,0:T(8,128)S(1)}, f32[3,1,64,128]{2,3,1,0:T(8,128)S(1)}, u32[]{:S(2)}, u32[]{:S(2)}) %collective-permute-start.1) | collective-permute-done | bytes 98336 | tf_op jit(solution)/shard_map/ppermute | solution.py:24
  42.5 6.0 %all_to_all.60 = f32[4,1,2048]{2,1,0:T(1,128)S(1)} all-to-all(f32[4,1,2048]{2,1,0:T(1,128)S(1)} %reshape.985), channel_id=1, replica_groups=mesh['gx'=8,'gy'=4] {'gy'}, dimensions={0} | all-to-all | bytes 65536 | tf_op jit(solution)/shard_map/all_to_all | solution.py:119
  48.4 0.7 reduce.13
  49.8 9.9 %while.21 = (s32[]{:T(128)}, f32[1,2,128,32]{2,3,1,0:T(8,128)S(1)}, f32[1,2,128,32]{2,3,1,0:T(8,128)S(1)}, f32[2]{0:T(128)S(1)}, f32[2]{0:T(128)S(1)}, /*index=5...) while((s32[]{:T(128)}, f32[1,2,128,32]{2,3,1,0:T(8,128)S(1)}, f32[1,2,128,32]{2,3,1,0:T(8,128)S(1)}, ...), condition=%wide.region_6.7_spmd, body=%wide.region_5.6_spmd.sunk | while | flops 12607618 | bytes 202597 | solution.py:83
  60.0 6.0 %all_to_all.61 = f32[4,1,2048]{2,1,0:T(1,128)S(1)} all-to-all(f32[4,1,2048]{2,1,0:T(1,128)S(1)} %reshape.987), channel_id=1, replica_groups=mesh['gx'=8,'gy'=4] {'gy'}, dimensions={0} | all-to-all | bytes 65536 | tf_op jit(solution)/shard_map/all_to_all | solution.py:124
  66.0 0.7 reduce.14
  66.8 2.0 %collective-permute-start.2 = (f32[3,1,64,128]{2,3,1,0:T(8,128)S(1)}, f32[3,1,64,128]{2,3,1,0:T(8,128)S(1)}, u32[]{:S(2)}, u32[]{:S(2)}) collective-permute-start(f32[3,1,64,128]{2,3,1,0:T(8,128)S(1)} %pad_maximum_fusion.9), channel_id=1, source_target_pairs={{4,0},{8,4},{12,8},{16,12},{20,16},{24,20},{28,24},{5,1},{9,5},{13... | collective-permute-start | bytes 294920 | tf_op jit(solution)/shard_map/ppermute | solution.py:25
  68.8 6.6 %collective-permute-start.3 = (f32[3,1,64,128]{2,3,1,0:T(8,128)S(1)}, f32[3,1,64,128]{2,3,1,0:T(8,128)S(1)}, u32[]{:S(2)}, u32[]{:S(2)}) collective-permute-start(f32[3,1,64,128]{2,3,1,0:T(8,128)S(1)} %pad_maximum_fusion.9), channel_id=1, source_target_pairs={{0,4},{4,8},{8,12},{12,16},{16,20},{20,24},{24,28},{1,5},{5,9},{9,... | collective-permute-start | bytes 294920 | tf_op jit(solution)/shard_map/ppermute | solution.py:24
  75.7 1.2 %collective-permute-done.2 = f32[3,1,64,128]{2,3,1,0:T(8,128)S(1)} collective-permute-done((f32[3,1,64,128]{2,3,1,0:T(8,128)S(1)}, f32[3,1,64,128]{2,3,1,0:T(8,128)S(1)}, u32[]{:S(2)}, u32[]{:S(2)}) %collective-permute-start.2) | collective-permute-done | bytes 98336 | tf_op jit(solution)/shard_map/ppermute | solution.py:25
  76.9 1.2 %collective-permute-done.3 = f32[3,1,64,128]{2,3,1,0:T(8,128)S(1)} collective-permute-done((f32[3,1,64,128]{2,3,1,0:T(8,128)S(1)}, f32[3,1,64,128]{2,3,1,0:T(8,128)S(1)}, u32[]{:S(2)}, u32[]{:S(2)}) %collective-permute-start.3) | collective-permute-done | bytes 98336 | tf_op jit(solution)/shard_map/ppermute | solution.py:24
  78.2 0.7 copy.94
  78.9 0.7 copy.95
  (261 shorter events, 25.9 us)
Async XLA Ops:
  2.2 4.4 %copy-start.5 = (f32[2]{0:T(128)S(1)}, f32[2]{0:T(128)}, u32[]{:S(2)}) copy-start(f32[2]{0:T(128)} %param.20) | copy-start | bytes 28
  2.2 5.1 %copy-start.2 = (bf16[2,1,64,128]{3,2,1,0:T(8,128)(2,1)S(1)}, bf16[2,1,64,128]{3,2,1,0:T(8,128)(2,1)}, u32[]{:S(2)}) copy-start(bf16[2,1,64,128]{3,2,1,0:T(8,128)(2,1)} %param.15) | copy-start | bytes 98308
  2.2 8.0 %all-to-all-start = ((f32[4,1,2048]{2,1,0:T(1,128)}), f32[4,1,2048]{2,1,0:T(1,128)S(1)}, u32[]{:S(2)}, u32[]{:S(2)}) async-start(f32[4,1,2048]{2,1,0:T(1,128)} %reshape.981), calls=%async_computation | async-start | bytes 65536 | tf_op jit(solution)/shard_map/all_to_all | solution.py:119
  6.6 0.7 copy-start.6
  7.3 0.8 copy-start.3
  9.3 0.7 copy-start.4
  9.4 0.7 copy-start.7
  11.6 0.9 %copy-start = (f32[2,128,128]{2,1,0:T(8,128)S(1)}, f32[2,128,128]{2,1,0:T(8,128)}, u32[]{:S(2)}) copy-start(f32[2,128,128]{2,1,0:T(8,128)} %param.21) | copy-start | bytes 393220
  23.6 7.2 %all-to-all-start.1 = ((f32[4,1,2048]{2,1,0:T(1,128)}), f32[4,1,2048]{2,1,0:T(1,128)S(1)}, u32[]{:S(2)}, u32[]{:S(2)}) async-start(f32[4,1,2048]{2,1,0:T(1,128)} %reshape.983), calls=%async_computation.1 | async-start | bytes 65536 | tf_op jit(solution)/shard_map/all_to_all | solution.py:124
  31.7 9.3 %collective-permute-start = (f32[3,1,64,128]{2,3,1,0:T(8,128)S(1)}, f32[3,1,64,128]{2,3,1,0:T(8,128)S(1)}, u32[]{:S(2)}, u32[]{:S(2)}) collective-permute-start(f32[3,1,64,128]{2,3,1,0:T(8,128)S(1)} %pad_maximum_fusion.8), channel_id=1, source_target_pairs={{4,0},{8,4},{12,8},{16,12},{20,16},{24,20},{28,24},{5,1},{9,5},{13... | collective-permute-start | bytes 294920 | tf_op jit(solution)/shard_map/ppermute | solution.py:25
  36.5 5.7 %collective-permute-start.1 = (f32[3,1,64,128]{2,3,1,0:T(8,128)S(1)}, f32[3,1,64,128]{2,3,1,0:T(8,128)S(1)}, u32[]{:S(2)}, u32[]{:S(2)}) collective-permute-start(f32[3,1,64,128]{2,3,1,0:T(8,128)S(1)} %pad_maximum_fusion.8), channel_id=1, source_target_pairs={{0,4},{4,8},{8,12},{12,16},{16,20},{20,24},{24,28},{1,5},{5,9},{9,... | collective-permute-start | bytes 294920 | tf_op jit(solution)/shard_map/ppermute | solution.py:24
  39.8 0.8 copy-start.1
  66.8 10.0 %collective-permute-start.2 = (f32[3,1,64,128]{2,3,1,0:T(8,128)S(1)}, f32[3,1,64,128]{2,3,1,0:T(8,128)S(1)}, u32[]{:S(2)}, u32[]{:S(2)}) collective-permute-start(f32[3,1,64,128]{2,3,1,0:T(8,128)S(1)} %pad_maximum_fusion.9), channel_id=1, source_target_pairs={{4,0},{8,4},{12,8},{16,12},{20,16},{24,20},{28,24},{5,1},{9,5},{13... | collective-permute-start | bytes 294920 | tf_op jit(solution)/shard_map/ppermute | solution.py:25
  68.8 9.2 %collective-permute-start.3 = (f32[3,1,64,128]{2,3,1,0:T(8,128)S(1)}, f32[3,1,64,128]{2,3,1,0:T(8,128)S(1)}, u32[]{:S(2)}, u32[]{:S(2)}) collective-permute-start(f32[3,1,64,128]{2,3,1,0:T(8,128)S(1)} %pad_maximum_fusion.9), channel_id=1, source_target_pairs={{0,4},{4,8},{8,12},{12,16},{16,20},{20,24},{24,28},{1,5},{5,9},{9,... | collective-permute-start | bytes 294920 | tf_op jit(solution)/shard_map/ppermute | solution.py:24
where the time goes:
time: 80.4 us; the launch traced here: 79.6 us
  starting transfers between devices  24.5 us (30%)
  local copies, waits for them, and re-layouts  19.2 us (24%)
  blocking collectives  11.9 us (15%)
  matrix products  8.49 us (11%)
  waiting for transfers between devices  7.58 us (9%)
  other arithmetic  5.04 us (6%)
  between operations  2.16 us (3%)
    ppermute x2, starting transfers between devices, with_halo(): before = lax.ppermute(last, axis, up)  9.73 us
    dot_general x22, matrix products, sweep_once(): jnp.einsum('bij,xbjy->xbiy', block_inverse, shaped + coupling, precision=...  7.89 us
    unnamed x32, local copies, waits for them, and re-layouts  7.66 us
    ppermute x2, starting transfers between devices, with_halo(): after = lax.ppermute(leading, axis, down)  6.77 us
    all_to_all x1, blocking collectives, per_device(): lax.all_to_all(outgoing, 'gy', split_axis=3, concat_axis=1, tiled=True)  5.96 us
    all_to_all x1, blocking collectives, per_device(): lax.all_to_all(returned_form, 'gy', split_axis=1, concat_axis=3, tiled=True)  5.96 us
    concatenate x88, local copies, waits for them, and re-layouts, sweep_once(): jnp.concatenate([from_below[:, :, None, :], middle, from_above[:, :, None...  5.81 us
    all_to_all x1, starting transfers between devices, per_device(): lax.all_to_all(outgoing, 'gy', split_axis=3, concat_axis=1, tiled=True)  4.4 us
  transfers between devices with their start and end apart: 6, of which 5 were waited for; matrix products, arithmetic and copies ran while one was open for 2% of the time, Pallas kernels for 0%

commit v1 on v0

--- a/solution.py
+++ b/solution.py
@@ -116,7 +116,20 @@
     for step_index in range(STEPS):
         later_index = STEPS - 1 - step_index
         outgoing = adjoint_v.reshape(row_count, 1, depth_cells, groups, narrow)
-        pieces = lax.all_to_all(outgoing, "gy", split_axis=3, concat_axis=1, tiled=True)
+        local_next = lax.axis_size("gy")
+        row_out = lax.axis_index("gy")
+        z1, near = (local_next, row_out)
+        outer = outgoing.shape[3] // z1
+        reached = list(outgoing.shape)
+        reached[3] = outer
+        f_now = reached[1]
+        reached[1] = f_now * z1
+        pieces = jnp.zeros(reached, outgoing.dtype)
+        for idx in range(z1):
+            x_new = lax.dynamic_slice_in_dim(outgoing, (near ^ idx) * outer, outer, axis=3)
+            if idx:
+                x_new = lax.ppermute(x_new, axis_name="gy", perm=[(d, d ^ idx) for d in range(z1)])
+            pieces = lax.dynamic_update_slice_in_dim(pieces, x_new, (near ^ idx) * f_now, axis=1)
         item_count = pieces.shape[0]
         line_cells = pieces.reshape(item_count, groups * depth_cells, narrow)
         solved_lines = line_solve(line_cells, block_rate, block_inverse)

time: 80.4 us -> 76.9 us (0.956)
  blocking collectives: 11.9 us -> 6.76 us
  starting transfers between devices: 24.5 us -> 27 us
  other arithmetic: 5.04 us -> 3.63 us
  waiting for transfers between devices: 7.58 us -> 8.68 us
    ppermute x0 -> x6, starting transfers between devices: none -> 6.09 us  [per_device(): lax.ppermute(x_new, axis_name='gy', perm=[(d, d ^ idx) for d in range(z1)])]
    all_to_all x1 -> x0, blocking collectives: 5.96 us -> none  [per_device(): lax.all_to_all(outgoing, 'gy', split_axis=3, concat_axis=1, tiled=True)]
    all_to_all x1 -> x0, starting transfers between devices: 4.4 us -> none  [per_device(): lax.all_to_all(outgoing, 'gy', split_axis=3, concat_axis=1, tiled=True)]
    all_to_all x2 -> x0, other arithmetic: 1.43 us -> none  [per_device(): lax.all_to_all(outgoing, 'gy', split_axis=3, concat_axis=1, tiled=True)]
    ppermute x0 -> x6, waiting for transfers between devices: none -> 1.12 us  [per_device(): lax.ppermute(x_new, axis_name='gy', perm=[(d, d ^ idx) for d in range(z1)])]
    unnamed x32 -> x28, local copies, waits for them, and re-layouts: 7.66 us -> 6.61 us
    ppermute x2, starting transfers between devices: 6.77 us -> 7.67 us  [with_halo(): after = lax.ppermute(leading, axis, down)]
  transfers between devices with their start and end apart: 6 -> 11, of which waited for: 5 -> 8; matrix products, arithmetic and copies ran while one was open for 2% -> 2% of each run, Pallas kernels for 0% -> 0%
where the time goes in v1:
time: 76.9 us; the launch traced here: 76.3 us
  starting transfers between devices  27 us (35%)
  local copies, waits for them, and re-layouts  18.8 us (24%)
  waiting for transfers between devices  8.68 us (11%)
  matrix products  8.49 us (11%)
  blocking collectives  6.76 us (9%)
  other arithmetic  3.63 us (5%)
  between operations  2.17 us (3%)
    ppermute x2, starting transfers between devices, with_halo(): before = lax.ppermute(last, axis, up)  9.73 us
    dot_general x22, matrix products, sweep_once(): jnp.einsum('bij,xbjy->xbiy', block_inverse, shaped + coupling, precision=...  7.89 us
    ppermute x2, starting transfers between devices, with_halo(): after = lax.ppermute(leading, axis, down)  7.67 us
    all_to_all x1, blocking collectives, per_device(): lax.all_to_all(returned_form, 'gy', split_axis=1, concat_axis=3, tiled=True)  6.76 us
    unnamed x28, local copies, waits for them, and re-layouts  6.61 us
    ppermute x6, starting transfers between devices, per_device(): lax.ppermute(x_new, axis_name='gy', perm=[(d, d ^ idx) for d in range(z1)])  6.09 us
    concatenate x88, local copies, waits for them, and re-layouts, sweep_once(): jnp.concatenate([from_below[:, :, None, :], middle, from_above[:, :, None...  5.81 us
    all_to_all x1, waiting for transfers between devices, per_device(): lax.all_to_all(returned_form, 'gy', split_axis=1, concat_axis=3, tiled=True)  3.6 us
  transfers between devices with their start and end apart: 11, of which 8 were waited for; matrix products, arithmetic and copies ran while one was open for 2% of the time, Pallas kernels for 0%

profile of v1, /device:TPU:1, one launch (start us, length us, event | category | flops | bytes accessed | tf_op | source)
XLA Modules:
  0.0 76.3 jit_solution(15313273844013842778)
XLA Ops:
  0.6 0.8 %copy.79 = f32[1,64,128]{1,2,0:T(8,128)S(1)} copy(f32[1,64,128]{2,1,0:T(8,128)} %param.13) | data formatting | bytes 65536 | tf_op args[0]
  1.6 2.1 %collective-permute-start = (f32[1,1,64,1,32]{2,4,3,1,0:T(8,128)S(1)}, f32[1,1,64,1,32]{2,4,3,1,0:T(8,128)S(1)}, u32[]{:S(2)}, u32[]{:S(2)}) collective-permute-start(f32[1,1,64,1,32]{2,4,3,1,0:T(8,128)S(1)} %get-tuple-element.163), channel_id=1, source_target_pairs={{0,1},{1,0},{2,3},{3,2},{4,5},{5,4},{6,7},{7,6},{8,9},{9,8},{10,11... | collective-permute-start | bytes 24584 | tf_op jit(solution)/shard_map/ppermute | solution.py:131
  3.7 1.2 %collective-permute-start.1 = (f32[1,1,64,1,32]{2,4,3,1,0:T(8,128)S(1)}, f32[1,1,64,1,32]{2,4,3,1,0:T(8,128)S(1)}, u32[]{:S(2)}, u32[]{:S(2)}) collective-permute-start(f32[1,1,64,1,32]{2,4,3,1,0:T(8,128)S(1)} %get-tuple-element.162), channel_id=1, source_target_pairs={{0,2},{1,3},{2,0},{3,1},{4,6},{5,7},{6,4},{7,5},{8,10},{9,11},{10,... | collective-permute-start | bytes 24584 | tf_op jit(solution)/shard_map/ppermute | solution.py:131
  5.6 0.7 copy-done.3
  9.1 0.7 copy-done
  10.1 9.9 %while.20 = (s32[]{:T(128)}, f32[1,2,128,32]{2,3,1,0:T(8,128)S(1)}, f32[1,2,128,32]{2,3,1,0:T(8,128)S(1)}, f32[2]{0:T(128)S(1)}, f32[2]{0:T(128)S(1)}, /*index=5...) while((s32[]{:T(128)}, f32[1,2,128,32]{2,3,1,0:T(8,128)S(1)}, f32[1,2,128,32]{2,3,1,0:T(8,128)S(1)}, ...), condition=%wide.region_1.2_spmd, body=%wide.region_0.1_spmd.sunk | while | flops 12607618 | bytes 202597 | solution.py:83
  20.1 0.7 reshape.979
  20.9 3.6 %all-to-all-start = ((f32[4,1,2048]{2,1,0:T(1,128)}), f32[4,1,2048]{2,1,0:T(1,128)S(1)}, u32[]{:S(2)}, u32[]{:S(2)}) async-start(f32[4,1,2048]{2,1,0:T(1,128)} %reshape.979), calls=%async_computation | async-start | bytes 65536 | tf_op jit(solution)/shard_map/all_to_all | solution.py:137
  24.4 3.6 %all-to-all-done = f32[4,1,2048]{2,1,0:T(1,128)S(1)} async-done(((f32[4,1,2048]{2,1,0:T(1,128)}), f32[4,1,2048]{2,1,0:T(1,128)S(1)}, u32[]{:S(2)}, u32[]{:S(2)}) %all-to-all-start) | async-done | bytes 32800 | tf_op jit(solution)/shard_map/all_to_all | solution.py:137
  28.5 0.7 reduce.11
  29.4 4.9 %collective-permute-start.3 = (f32[3,1,64,128]{2,3,1,0:T(8,128)S(1)}, f32[3,1,64,128]{2,3,1,0:T(8,128)S(1)}, u32[]{:S(2)}, u32[]{:S(2)}) collective-permute-start(f32[3,1,64,128]{2,3,1,0:T(8,128)S(1)} %pad_maximum_fusion.8), channel_id=1, source_target_pairs={{4,0},{8,4},{12,8},{16,12},{20,16},{24,20},{28,24},{5,1},{9,5},{13... | collective-permute-start | bytes 294920 | tf_op jit(solution)/shard_map/ppermute | solution.py:25
  34.3 3.1 %collective-permute-start.4 = (f32[3,1,64,128]{2,3,1,0:T(8,128)S(1)}, f32[3,1,64,128]{2,3,1,0:T(8,128)S(1)}, u32[]{:S(2)}, u32[]{:S(2)}) collective-permute-start(f32[3,1,64,128]{2,3,1,0:T(8,128)S(1)} %pad_maximum_fusion.8), channel_id=1, source_target_pairs={{0,4},{4,8},{8,12},{12,16},{16,20},{20,24},{24,28},{1,5},{5,9},{9,... | collective-permute-start | bytes 294920 | tf_op jit(solution)/shard_map/ppermute | solution.py:24
  38.8 1.2 %collective-permute-done.4 = f32[3,1,64,128]{2,3,1,0:T(8,128)S(1)} collective-permute-done((f32[3,1,64,128]{2,3,1,0:T(8,128)S(1)}, f32[3,1,64,128]{2,3,1,0:T(8,128)S(1)}, u32[]{:S(2)}, u32[]{:S(2)}) %collective-permute-start.4) | collective-permute-done | bytes 98336 | tf_op jit(solution)/shard_map/ppermute | solution.py:24
  40.8 2.1 %collective-permute-start.7 = (f32[1,1,64,1,32]{2,4,3,1,0:T(8,128)S(1)}, f32[1,1,64,1,32]{2,4,3,1,0:T(8,128)S(1)}, u32[]{:S(2)}, u32[]{:S(2)}) collective-permute-start(f32[1,1,64,1,32]{2,4,3,1,0:T(8,128)S(1)} %get-tuple-element.154), channel_id=1, source_target_pairs={{0,3},{1,2},{2,1},{3,0},{4,7},{5,6},{6,5},{7,4},{8,11},{9,10},{10,... | collective-permute-start | bytes 24584 | tf_op jit(solution)/shard_map/ppermute | solution.py:131
  43.4 0.8 %collective-permute-done.7 = f32[1,1,64,1,32]{2,4,3,1,0:T(8,128)S(1)} collective-permute-done((f32[1,1,64,1,32]{2,4,3,1,0:T(8,128)S(1)}, f32[1,1,64,1,32]{2,4,3,1,0:T(8,128)S(1)}, u32[]{:S(2)}, u32[]{:S(2)}) %collective-permute-start.7) | collective-permute-done | bytes 8224 | tf_op jit(solution)/shard_map/ppermute | solution.py:131
  44.9 9.9 %while.21 = (s32[]{:T(128)}, f32[1,2,128,32]{2,3,1,0:T(8,128)S(1)}, f32[1,2,128,32]{2,3,1,0:T(8,128)S(1)}, f32[2]{0:T(128)S(1)}, f32[2]{0:T(128)S(1)}, /*index=5...) while((s32[]{:T(128)}, f32[1,2,128,32]{2,3,1,0:T(8,128)S(1)}, f32[1,2,128,32]{2,3,1,0:T(8,128)S(1)}, ...), condition=%wide.region_6.7_spmd, body=%wide.region_5.6_spmd.sunk | while | flops 12607618 | bytes 202597 | solution.py:83
  55.0 6.8 %all_to_all.30 = f32[4,1,2048]{2,1,0:T(1,128)S(1)} all-to-all(f32[4,1,2048]{2,1,0:T(1,128)S(1)} %reshape.981), channel_id=1, replica_groups=mesh['gx'=8,'gy'=4] {'gy'}, dimensions={0} | all-to-all | bytes 65536 | tf_op jit(solution)/shard_map/all_to_all | solution.py:137
  61.8 0.7 reduce.12
  62.7 2.8 %collective-permute-start.8 = (f32[3,1,64,128]{2,3,1,0:T(8,128)S(1)}, f32[3,1,64,128]{2,3,1,0:T(8,128)S(1)}, u32[]{:S(2)}, u32[]{:S(2)}) collective-permute-start(f32[3,1,64,128]{2,3,1,0:T(8,128)S(1)} %pad_maximum_fusion.9), channel_id=1, source_target_pairs={{4,0},{8,4},{12,8},{16,12},{20,16},{24,20},{28,24},{5,1},{9,5},{13... | collective-permute-start | bytes 294920 | tf_op jit(solution)/shard_map/ppermute | solution.py:25
  65.5 6.6 %collective-permute-start.9 = (f32[3,1,64,128]{2,3,1,0:T(8,128)S(1)}, f32[3,1,64,128]{2,3,1,0:T(8,128)S(1)}, u32[]{:S(2)}, u32[]{:S(2)}) collective-permute-start(f32[3,1,64,128]{2,3,1,0:T(8,128)S(1)} %pad_maximum_fusion.9), channel_id=1, source_target_pairs={{0,4},{4,8},{8,12},{12,16},{16,20},{20,24},{24,28},{1,5},{5,9},{9,... | collective-permute-start | bytes 294920 | tf_op jit(solution)/shard_map/ppermute | solution.py:24
  72.4 1.2 %collective-permute-done.8 = f32[3,1,64,128]{2,3,1,0:T(8,128)S(1)} collective-permute-done((f32[3,1,64,128]{2,3,1,0:T(8,128)S(1)}, f32[3,1,64,128]{2,3,1,0:T(8,128)S(1)}, u32[]{:S(2)}, u32[]{:S(2)}) %collective-permute-start.8) | collective-permute-done | bytes 98336 | tf_op jit(solution)/shard_map/ppermute | solution.py:25
  73.6 1.2 %collective-permute-done.9 = f32[3,1,64,128]{2,3,1,0:T(8,128)S(1)} collective-permute-done((f32[3,1,64,128]{2,3,1,0:T(8,128)S(1)}, f32[3,1,64,128]{2,3,1,0:T(8,128)S(1)}, u32[]{:S(2)}, u32[]{:S(2)}) %collective-permute-start.9) | collective-permute-done | bytes 98336 | tf_op jit(solution)/shard_map/ppermute | solution.py:24
  74.9 0.7 copy.102
  75.6 0.7 copy.103
  (272 shorter events, 26.5 us)
Async XLA Ops:
  1.5 4.1 %copy-start.2 = (bf16[2,1,64,128]{3,2,1,0:T(8,128)(2,1)S(1)}, bf16[2,1,64,128]{3,2,1,0:T(8,128)(2,1)}, u32[]{:S(2)}) copy-start(bf16[2,1,64,128]{3,2,1,0:T(8,128)(2,1)} %param.15) | copy-start | bytes 98308
  1.6 7.0 %collective-permute-start = (f32[1,1,64,1,32]{2,4,3,1,0:T(8,128)S(1)}, f32[1,1,64,1,32]{2,4,3,1,0:T(8,128)S(1)}, u32[]{:S(2)}, u32[]{:S(2)}) collective-permute-start(f32[1,1,64,1,32]{2,4,3,1,0:T(8,128)S(1)} %get-tuple-element.163), channel_id=1, source_target_pairs={{0,1},{1,0},{2,3},{3,2},{4,5},{5,4},{6,7},{7,6},{8,9},{9,8},{10,11... | collective-permute-start | bytes 24584 | tf_op jit(solution)/shard_map/ppermute | solution.py:131
  3.7 1.3 %copy-start.5 = (f32[2]{0:T(128)S(1)}, f32[2]{0:T(128)}, u32[]{:S(2)}) copy-start(f32[2]{0:T(128)} %param.20) | copy-start | bytes 28
  3.7 5.0 %collective-permute-start.1 = (f32[1,1,64,1,32]{2,4,3,1,0:T(8,128)S(1)}, f32[1,1,64,1,32]{2,4,3,1,0:T(8,128)S(1)}, u32[]{:S(2)}, u32[]{:S(2)}) collective-permute-start(f32[1,1,64,1,32]{2,4,3,1,0:T(8,128)S(1)} %get-tuple-element.162), channel_id=1, source_target_pairs={{0,2},{1,3},{2,0},{3,1},{4,6},{5,7},{6,4},{7,5},{8,10},{9,11},{10,... | collective-permute-start | bytes 24584 | tf_op jit(solution)/shard_map/ppermute | solution.py:131
  4.9 0.7 copy-start.6
  4.9 3.8 %collective-permute-start.2 = (f32[1,1,64,1,32]{2,4,3,1,0:T(8,128)S(1)}, f32[1,1,64,1,32]{2,4,3,1,0:T(8,128)S(1)}, u32[]{:S(2)}, u32[]{:S(2)}) collective-permute-start(f32[1,1,64,1,32]{2,4,3,1,0:T(8,128)S(1)} %get-tuple-element.161), channel_id=1, source_target_pairs={{0,3},{1,2},{2,1},{3,0},{4,7},{5,6},{6,5},{7,4},{8,11},{9,10},{10,... | collective-permute-start | bytes 24584 | tf_op jit(solution)/shard_map/ppermute | solution.py:131
  5.6 0.8 copy-start.3
  7.6 0.7 copy-start.4
  7.6 0.7 copy-start.7
  8.8 0.9 %copy-start = (f32[2,128,128]{2,1,0:T(8,128)S(1)}, f32[2,128,128]{2,1,0:T(8,128)}, u32[]{:S(2)}) copy-start(f32[2,128,128]{2,1,0:T(8,128)} %param.21) | copy-start | bytes 393220
  20.9 7.2 %all-to-all-start = ((f32[4,1,2048]{2,1,0:T(1,128)}), f32[4,1,2048]{2,1,0:T(1,128)S(1)}, u32[]{:S(2)}, u32[]{:S(2)}) async-start(f32[4,1,2048]{2,1,0:T(1,128)} %reshape.979), calls=%async_computation | async-start | bytes 65536 | tf_op jit(solution)/shard_map/all_to_all | solution.py:137
  29.4 9.4 %collective-permute-start.3 = (f32[3,1,64,128]{2,3,1,0:T(8,128)S(1)}, f32[3,1,64,128]{2,3,1,0:T(8,128)S(1)}, u32[]{:S(2)}, u32[]{:S(2)}) collective-permute-start(f32[3,1,64,128]{2,3,1,0:T(8,128)S(1)} %pad_maximum_fusion.8), channel_id=1, source_target_pairs={{4,0},{8,4},{12,8},{16,12},{20,16},{24,20},{28,24},{5,1},{9,5},{13... | collective-permute-start | bytes 294920 | tf_op jit(solution)/shard_map/ppermute | solution.py:25
  34.3 5.7 %collective-permute-start.4 = (f32[3,1,64,128]{2,3,1,0:T(8,128)S(1)}, f32[3,1,64,128]{2,3,1,0:T(8,128)S(1)}, u32[]{:S(2)}, u32[]{:S(2)}) collective-permute-start(f32[3,1,64,128]{2,3,1,0:T(8,128)S(1)} %pad_maximum_fusion.8), channel_id=1, source_target_pairs={{0,4},{4,8},{8,12},{12,16},{16,20},{20,24},{24,28},{1,5},{5,9},{9,... | collective-permute-start | bytes 294920 | tf_op jit(solution)/shard_map/ppermute | solution.py:24
  37.5 0.8 %copy-start.1 = (f32[1,64,128]{2,1,0:T(8,128)S(1)}, f32[1,64,128]{2,1,0:T(8,128)}, u32[]{:S(2)}) copy-start(f32[1,64,128]{2,1,0:T(8,128)} %param.14) | copy-start | bytes 98308
  40.1 2.9 %collective-permute-start.5 = (f32[1,1,64,1,32]{2,4,3,1,0:T(8,128)S(1)}, f32[1,1,64,1,32]{2,4,3,1,0:T(8,128)S(1)}, u32[]{:S(2)}, u32[]{:S(2)}) collective-permute-start(f32[1,1,64,1,32]{2,4,3,1,0:T(8,128)S(1)} %get-tuple-element.156), channel_id=1, source_target_pairs={{0,1},{1,0},{2,3},{3,2},{4,5},{5,4},{6,7},{7,6},{8,9},{9,8},{10,11... | collective-permute-start | bytes 24584 | tf_op jit(solution)/shard_map/ppermute | solution.py:131
  40.6 2.8 %collective-permute-start.6 = (f32[1,1,64,1,32]{2,4,3,1,0:T(8,128)S(1)}, f32[1,1,64,1,32]{2,4,3,1,0:T(8,128)S(1)}, u32[]{:S(2)}, u32[]{:S(2)}) collective-permute-start(f32[1,1,64,1,32]{2,4,3,1,0:T(8,128)S(1)} %get-tuple-element.155), channel_id=1, source_target_pairs={{0,2},{1,3},{2,0},{3,1},{4,6},{5,7},{6,4},{7,5},{8,10},{9,11},{10,... | collective-permute-start | bytes 24584 | tf_op jit(solution)/shard_map/ppermute | solution.py:131
  40.8 3.5 %collective-permute-start.7 = (f32[1,1,64,1,32]{2,4,3,1,0:T(8,128)S(1)}, f32[1,1,64,1,32]{2,4,3,1,0:T(8,128)S(1)}, u32[]{:S(2)}, u32[]{:S(2)}) collective-permute-start(f32[1,1,64,1,32]{2,4,3,1,0:T(8,128)S(1)} %get-tuple-element.154), channel_id=1, source_target_pairs={{0,3},{1,2},{2,1},{3,0},{4,7},{5,6},{6,5},{7,4},{8,11},{9,10},{10,... | collective-permute-start | bytes 24584 | tf_op jit(solution)/shard_map/ppermute | solution.py:131
  62.7 10.9 %collective-permute-start.8 = (f32[3,1,64,128]{2,3,1,0:T(8,128)S(1)}, f32[3,1,64,128]{2,3,1,0:T(8,128)S(1)}, u32[]{:S(2)}, u32[]{:S(2)}) collective-permute-start(f32[3,1,64,128]{2,3,1,0:T(8,128)S(1)} %pad_maximum_fusion.9), channel_id=1, source_target_pairs={{4,0},{8,4},{12,8},{16,12},{20,16},{24,20},{28,24},{5,1},{9,5},{13... | collective-permute-start | bytes 294920 | tf_op jit(solution)/shard_map/ppermute | solution.py:25
  65.5 9.2 %collective-permute-start.9 = (f32[3,1,64,128]{2,3,1,0:T(8,128)S(1)}, f32[3,1,64,128]{2,3,1,0:T(8,128)S(1)}, u32[]{:S(2)}, u32[]{:S(2)}) collective-permute-start(f32[3,1,64,128]{2,3,1,0:T(8,128)S(1)} %pad_maximum_fusion.9), channel_id=1, source_target_pairs={{0,4},{4,8},{8,12},{12,16},{16,20},{20,24},{24,28},{1,5},{5,9},{9,... | collective-permute-start | bytes 294920 | tf_op jit(solution)/shard_map/ppermute | solution.py:24
